TPU v7x, 512 devices: a whole 4x8x8 slice. The times are simulated.
512 devices in a mesh: grp: 16 (over z, y_lo), col: 32 (over x, y_hi, core).
Axes of the slice: x: 4, y: 8 (y_hi: 4, y_lo: 2; y = y_hi * 2 + y_lo), z: 8, core: 2. Of those that a mesh axis runs over, the one named last changes fastest.
Arguments:
- descriptors: bfloat16 [10, 32, 128, 4096], P(None, None, 'grp', 'col'), may hold values from -6 to 6
- solid_temp: float32 [32, 128, 4096], P(None, 'grp', 'col'), may hold values from -6 to 6
- fluid_temp: float32 [32, 128, 4096], P(None, 'grp', 'col'), may hold values from -6 to 6
- material: int32 [32, 128, 4096], P(None, 'grp', 'col'), may hold values from 0 to 3
- fixed_mask: int32 [32, 128, 4096], P(None, 'grp', 'col'), may hold values 0 or 1
- solid_cond: float32 [4], replicated, may hold values from 0.3 to 1.5
- fluid_cond: float32 [4], replicated, may hold values from 0.3 to 1.5
- w_in: bfloat16 [12, 64], replicated, may hold values from -1.75 to 1.75
- b_in: float32 [64], replicated, may hold values from -3 to 3
- w_mid: bfloat16 [64, 64], replicated, may hold values from -0.75 to 0.75
- b_mid: float32 [64], replicated, may hold values from -3 to 3
- w_out: bfloat16 [64, 2], replicated, may hold values from -0.75 to 0.75
- b_out: float32 [2], replicated, may hold values from -3 to 3
- solid_cot: float32 [32, 128, 4096], P(None, 'grp', 'col'), may hold values from -18 to 18
- fluid_cot: float32 [32, 128, 4096], P(None, 'grp', 'col'), may hold values from -18 to 18
Outputs:
- adj_solid: float32 [32, 128, 4096], P(None, 'grp', 'col')
- adj_fluid: float32 [32, 128, 4096], P(None, 'grp', 'col')
- grad_w_in: float32 [12, 64], replicated
- grad_b_in: float32 [64], replicated
- grad_w_mid: float32 [64, 64], replicated
- grad_b_mid: float32 [64], replicated
- grad_w_out: float32 [64, 2], replicated
- grad_b_out: float32 [2], replicated
All inputs are finite; a program needn't handle non-finite values. No bound on the sum of `fixed_mask` on one device may be relied on, other than what follows from the above.
Results may differ from a plain program's by a relative error of at most 0.01.
The roundings to bfloat16 on the way count: a program that leaves them out, or rounds other values in their place, can miss the bound.
Values sent between devices are 32-bit elements; how exact they have to be, the bound alone decides.
No kernel may reach another device: no remote copies, remote signals or barrier semaphores. Data moves between devices by JAX's collectives and lax.ppermute only.
A program may use at most 64 MiB of HBM per device.

v0:
```python
import math
import jax
import jax.numpy as jnp
from jax import lax
from jax.sharding import PartitionSpec as P

time_step = 0.15
loss_gain = 16.0


def padded_2(block, sides, width):
    for axis, dim in sides:
        count = lax.axis_size(axis)
        forward = [(i, i + 1) for i in range(count - 1)]
        backward = [(target, source) for source, target in forward]
        low = lax.ppermute(
            lax.slice_in_dim(block, block.shape[dim] - width, None, axis=dim), axis, forward
        )
        high = lax.ppermute(lax.slice_in_dim(block, 0, width, axis=dim), axis, backward)
        block = jnp.concatenate([low, block, high], axis=dim)
    return block


def material_lookup(material, lookup_table):
    summed = jnp.zeros(material.shape, jnp.float32)
    for material_kind in range(lookup_table.shape[0]):
        summed = summed + jnp.where(material == material_kind, lookup_table[material_kind], 0.0)
    return summed


def neighbour_sum(padded, values_field):
    return (
        padded[:, :, 2:, 1:-1]
        + padded[:, :, :-2, 1:-1]
        + padded[:, :, 1:-1, 2:]
        + padded[:, :, 1:-1, :-2]
        - 4.0 * values_field
    )


def network(features, w_in, b_in, w_mid, b_mid, w_out, b_out):
    hidden_one = jnp.tanh(
        jnp.dot(w_in.T, features, preferred_element_type=jnp.float32) + b_in[:, None]
    ).astype(jnp.bfloat16)
    hidden_two = jnp.tanh(
        jnp.dot(w_mid.T, hidden_one, preferred_element_type=jnp.float32) + b_mid[:, None]
    ).astype(jnp.bfloat16)
    logits = jnp.dot(w_out.T, hidden_two, preferred_element_type=jnp.float32) + b_out[:, None]
    return (hidden_one, hidden_two, logits)


def coupling_terms(logits):
    transfer_coef = jax.nn.softplus(logits[0])
    area_coef = jax.nn.softplus(logits[1])
    return (transfer_coef * area_coef, transfer_coef, area_coef)


def backprop(features, hidden_one, hidden_two, logits, d_coupling, w_in, w_mid, w_out):
    coupling, transfer_coef, area_coef = coupling_terms(logits)
    d_logits = jnp.stack(
        [
            d_coupling * area_coef * jax.nn.sigmoid(logits[0]),
            d_coupling * transfer_coef * jax.nn.sigmoid(logits[1]),
        ]
    ).astype(jnp.bfloat16)
    d_hidden_two = (
        jnp.dot(w_out, d_logits, preferred_element_type=jnp.float32)
        * (1.0 - jnp.square(hidden_two.astype(jnp.float32)))
    ).astype(jnp.bfloat16)
    d_hidden_one = (
        jnp.dot(w_mid, d_hidden_two, preferred_element_type=jnp.float32)
        * (1.0 - jnp.square(hidden_one.astype(jnp.float32)))
    ).astype(jnp.bfloat16)
    d_features = jnp.dot(
        w_in[w_in.shape[0] - 2 :], d_hidden_one, preferred_element_type=jnp.float32
    )
    gradients = (
        jnp.dot(features, d_hidden_one.T, preferred_element_type=jnp.float32),
        jnp.sum(d_hidden_one.astype(jnp.float32), axis=1),
        jnp.dot(hidden_one, d_hidden_two.T, preferred_element_type=jnp.float32),
        jnp.sum(d_hidden_two.astype(jnp.float32), axis=1),
        jnp.dot(hidden_two, d_logits.T, preferred_element_type=jnp.float32),
        jnp.sum(d_logits.astype(jnp.float32), axis=1),
    )
    return (coupling, d_features, gradients)


def build_features(desc_line, solid_line, fluid_line):
    cells = solid_line.size
    return jnp.concatenate(
        [
            desc_line.reshape(desc_line.shape[0], cells),
            solid_line.reshape(1, cells).astype(jnp.bfloat16),
            fluid_line.reshape(1, cells).astype(jnp.bfloat16),
        ],
        axis=0,
    )


def forward_coupling(descriptors, solid, fluid, weights):

    def forward_one_line(line_index):
        desc_line = lax.dynamic_index_in_dim(descriptors, line_index, 1, keepdims=False)
        solid_line = lax.dynamic_index_in_dim(solid, line_index, 0, keepdims=False)
        fluid_line = lax.dynamic_index_in_dim(fluid, line_index, 0, keepdims=False)
        features = build_features(desc_line, solid_line, fluid_line)
        logits = network(features, *weights)[2]
        return coupling_terms(logits)[0].reshape(solid_line.shape)

    return lax.map(forward_one_line, jnp.arange(solid.shape[0], dtype=jnp.int32))


def backward_lines(descriptors, solid, fluid, d_coupling, weights, running):
    w_in, b_in, w_mid, b_mid, w_out, b_out = weights

    def backward_one_line(running, line_index):
        desc_line = lax.dynamic_index_in_dim(descriptors, line_index, 1, keepdims=False)
        solid_line = lax.dynamic_index_in_dim(solid, line_index, 0, keepdims=False)
        fluid_line = lax.dynamic_index_in_dim(fluid, line_index, 0, keepdims=False)
        d_line = lax.dynamic_index_in_dim(d_coupling, line_index, 0, keepdims=False)
        features = build_features(desc_line, solid_line, fluid_line)
        hidden_one, hidden_two, logits = network(features, *weights)
        coupling, d_features, gradients = backprop(
            features, hidden_one, hidden_two, logits, d_line.reshape(-1), w_in, w_mid, w_out
        )
        running = tuple((left + right for left, right in zip(running, gradients)))
        line_shape = solid_line.shape
        return (running, (coupling.reshape(line_shape), d_features.reshape((2,) + line_shape)))

    running, (coupling, d_features) = lax.scan(
        backward_one_line, running, jnp.arange(solid.shape[0], dtype=jnp.int32)
    )
    return (running, coupling, jnp.moveaxis(d_features, 1, 0))


def advance(state, state_padded, conduct, free_cell, first_coupling):
    coupled = first_coupling * (state[1] - state[0])
    return state + time_step * free_cell * (
        conduct * neighbour_sum(state_padded, state) + jnp.stack([coupled, -coupled])
    )


def shards(
    descriptors,
    solid_temp,
    fluid_temp,
    material,
    fixed_mask,
    solid_cond,
    fluid_cond,
    w_in,
    b_in,
    w_mid,
    b_mid,
    w_out,
    b_out,
    solid_cot,
    fluid_cot,
):
    weights = (w_in, b_in, w_mid, b_mid, w_out, b_out)
    conduct = jnp.stack(
        [material_lookup(material, solid_cond), material_lookup(material, fluid_cond)]
    )
    free_cell = 1.0 - fixed_mask.astype(jnp.float32)
    state = jnp.stack([solid_temp, fluid_temp])
    first_coupling = forward_coupling(descriptors, state[0], state[1], weights)
    cotangent = jnp.stack([solid_cot, fluid_cot])
    upstream = time_step * free_cell * cotangent
    pushed = conduct * upstream
    state_padded = padded_2(state, (("grp", 2), ("col", 3)), 1)
    later = advance(state, state_padded, conduct, free_cell, first_coupling)
    pushed_rim = padded_2(pushed, (("grp", 2), ("col", 3)), 1)
    running = (
        jnp.zeros(w_in.shape, jnp.float32),
        jnp.zeros(b_in.shape, jnp.float32),
        jnp.zeros(w_mid.shape, jnp.float32),
        jnp.zeros(b_mid.shape, jnp.float32),
        jnp.zeros(w_out.shape, jnp.float32),
        jnp.zeros(b_out.shape, jnp.float32),
    )
    d_coupling = (later[1] - later[0]) * (upstream[0] - upstream[1])
    running, coupling, d_features = backward_lines(
        descriptors, later[0], later[1], d_coupling, weights, running
    )
    swing_term = coupling * (upstream[1] - upstream[0])
    cotangent = (
        cotangent
        + neighbour_sum(pushed_rim, pushed)
        + jnp.stack([swing_term, -swing_term])
        + d_features
    )
    upstream = time_step * free_cell * cotangent
    pushed = conduct * upstream
    pushed_rim = padded_2(pushed, (("grp", 2), ("col", 3)), 1)
    d_coupling = (state[1] - state[0]) * (upstream[0] - upstream[1])
    running, coupling, d_features = backward_lines(
        descriptors, state[0], state[1], d_coupling, weights, running
    )
    swing_term = coupling * (upstream[1] - upstream[0])
    cotangent = (
        cotangent
        + neighbour_sum(pushed_rim, pushed)
        + jnp.stack([swing_term, -swing_term])
        + d_features
    )
    summed = lax.psum(
        (running[0], running[1], running[2], running[3], running[4], running[5]), ("grp", "col")
    )
    cell_count = solid_temp.size * lax.axis_size("grp") * lax.axis_size("col")
    scale = loss_gain / math.sqrt(cell_count)
    return (
        cotangent[0],
        cotangent[1],
        summed[0] * scale,
        summed[1] * scale,
        summed[2] * scale,
        summed[3] * scale,
        summed[4] * scale,
        summed[5] * scale,
    )


def solution(mesh):
    placed = (
        P(None, None, "grp", "col"),
        P(None, "grp", "col"),
        P(None, "grp", "col"),
        P(None, "grp", "col"),
        P(None, "grp", "col"),
        P(),
        P(),
        P(),
        P(),
        P(),
        P(),
        P(),
        P(),
        P(None, "grp", "col"),
        P(None, "grp", "col"),
    )
    return jax.shard_map(
        shards,
        mesh=mesh,
        in_specs=placed,
        out_specs=(P(None, "grp", "col"), P(None, "grp", "col"), P(), P(), P(), P(), P(), P()),
        check_vma=False,
    )
```

profile of v0, /device:TPU:19, one launch (start us, length us, event | category | flops | bytes accessed | tf_op | source)
XLA Modules:
  0.0 927.6 jit_solution(6519059867842374332)
XLA Ops:
  0.7 1.2 fusion.89
  1.9 1.3 collective-permute-start.4
  3.2 4.0 collective-permute-start.5
  8.4 2.7 add_bitcast_fusion.1
  11.1 2.7 add_bitcast_fusion
  14.0 1.3 collective-permute-start
  15.3 4.7 collective-permute-start.1
  20.8 128.7 %while.59 = (s32[]{:T(128)}, f32[32,8,128]{2,1,0:T(8,128)S(1)}, s32[32]{0:T(128)S(1)}, bf16[10,32,8,128]{3,2,1,0:T(8,128)(2,1)}, bf16[32,8,128]{2,1,0:T(8,128)(2...) while((s32[]{:T(128)}, f32[32,8,128]{2,1,0:T(8,128)S(1)}, ...), condition=%wide.region_1.2_spmd, body=%wide.region_0.1_spmd.sunk | while | flops 10574853 | bytes 510433 | solution.py:110
  150.6 6.4 collective-permute-start.7
  157.0 1.9 collective-permute-start.6
  159.6 1.2 fusion.96
  160.7 5.7 collective-permute-start.3
  166.5 1.9 collective-permute-start.2
  168.4 2.3 collective-permute-done.7
  170.7 1.9 collective-permute-done.6
  173.7 415.8 %while.61 = (s32[]{:T(128)}, f32[12,64]{1,0:T(8,128)S(1)}, f32[64]{0:T(128)}, f32[64,64]{1,0:T(8,128)S(1)}, f32[64]{0:T(128)}, /*index=5*/f32[64,2]{0,1:T(2,128)...) while((s32[]{:T(128)}, f32[12,64]{1,0:T(8,128)S(1)}, ...), condition=%wide.region_6.7_spmd.clone, body=%wide.region_2.6_spmd.clone.sunk | while | flops 30749576 | bytes 3280900 | solution.py:130
  177.4 0.9 fusion.247
  180.1 0.9 convert_reduce_fusion.16
  190.4 0.9 fusion.247
  193.1 0.9 convert_reduce_fusion.16
  203.4 0.9 fusion.247
  206.0 0.9 convert_reduce_fusion.16
  216.4 0.9 fusion.247
  219.0 0.9 convert_reduce_fusion.16
  229.4 0.9 fusion.247
  232.0 0.9 convert_reduce_fusion.16
  242.4 0.9 fusion.247
  245.0 0.9 convert_reduce_fusion.16
  255.4 0.9 fusion.247
  258.0 0.9 convert_reduce_fusion.16
  268.4 0.9 fusion.247
  271.0 0.9 convert_reduce_fusion.16
  284.0 0.9 convert_reduce_fusion.16
  297.0 0.9 convert_reduce_fusion.16
  310.0 0.9 convert_reduce_fusion.16
  323.0 0.9 convert_reduce_fusion.16
  336.0 0.9 convert_reduce_fusion.16
  349.0 0.9 convert_reduce_fusion.16
  362.0 0.9 convert_reduce_fusion.16
  375.0 0.9 convert_reduce_fusion.16
  388.0 0.9 convert_reduce_fusion.16
  401.0 0.9 convert_reduce_fusion.16
  413.9 0.9 convert_reduce_fusion.16
  426.9 0.9 convert_reduce_fusion.16
  439.9 0.9 convert_reduce_fusion.16
  452.9 0.9 convert_reduce_fusion.16
  465.9 0.9 convert_reduce_fusion.16
  478.9 0.9 convert_reduce_fusion.16
  491.9 0.9 convert_reduce_fusion.16
  504.9 0.9 convert_reduce_fusion.16
  517.9 0.9 convert_reduce_fusion.16
  530.9 0.9 convert_reduce_fusion.16
  543.9 0.9 convert_reduce_fusion.16
  556.9 0.9 convert_reduce_fusion.16
  569.9 0.9 convert_reduce_fusion.16
  582.9 0.9 convert_reduce_fusion.16
  591.3 1.3 collective-permute-start.8
  592.6 5.6 collective-permute-start.9
  599.1 195.9 %while.60 = (s32[]{:T(128)}, f32[12,64]{1,0:T(8,128)S(1)}, f32[64]{0:T(128)S(1)}, f32[64,64]{1,0:T(8,128)S(1)}, f32[64]{0:T(128)S(1)}, /*index=5*/f32[64,2]{0,1:...) while((s32[]{:T(128)}, f32[12,64]{1,0:T(8,128)S(1)}, ...), condition=%wide.region_11.12_spmd, body=%wide.region_7.11_spmd.sunk | while | flops 30744452 | bytes 2216265 | solution.py:130
  795.1 105.4 %all-reduce = (f32[12,64]{1,0:T(8,128)S(1)}, f32[64]{0:T(128)S(1)}, f32[64,64]{1,0:T(8,128)S(1)}, f32[64]{0:T(128)S(1)}, f32[64,2]{0,1:T(2,128)S(1)}, /*index=5*/f32[2]{0:T(128)S(1)}) all-reduce(f32[12,64]{1,0:T(8,128)S(1)} %get-tuple-element.299, f32[64]{0:T(128)S(1)} %get-tuple-element.300, ...), channel_id=1, replica_groups=mesh['grp'=16,'col'=32] {'grp','col'}, use_global_device_ids=true, to_apply=%region_12.13 | all-reduce | flops 5122 | bytes 40976 | tf_op jit(solution)/shard_map/psum | solution.py:206
  903.6 5.0 collective-permute-start.11
  908.5 1.9 collective-permute-start.10
  911.0 9.3 collective-permute-done.11
  920.2 6.3 collective-permute-done.10
  (3296 shorter events, 527.5 us)
Async XLA Ops:
  0.6 7.8 copy-start.7
  0.6 7.8 copy-start.8
  1.8 5.3 copy-start.31
  1.9 148.4 %collective-permute-start.4 = (f32[2,32,1,128]{3,2,1,0:T(1,128)S(1)}, f32[2,32,1,128]{3,2,1,0:T(1,128)S(1)}, u32[]{:S(2)}, u32[]{:S(2)}) collective-permute-start(f32[2,32,1,128]{3,2,1,0:T(1,128)S(1)} %get-tuple-element.537), channel_id=1, source_target_pairs={{32,0},{64,32},{96,64},{128,96},{160,128},{192,160},{224,192},{256... | collective-permute-start | bytes 98312 | tf_op jit(solution)/shard_map/ppermute | solution.py:19
  3.2 147.1 %collective-permute-start.5 = (f32[2,32,1,128]{3,2,1,0:T(1,128)S(1)}, f32[2,32,1,128]{3,2,1,0:T(1,128)S(1)}, u32[]{:S(2)}, u32[]{:S(2)}) collective-permute-start(f32[2,32,1,128]{3,2,1,0:T(1,128)S(1)} %get-tuple-element.536), channel_id=1, source_target_pairs={{0,32},{32,64},{64,96},{96,128},{128,160},{160,192},{192,224},{224... | collective-permute-start | bytes 98312 | tf_op jit(solution)/shard_map/ppermute | solution.py:16
  13.9 6.2 copy-start.1
  13.9 6.1 copy-start
  14.0 144.9 %collective-permute-start = (f32[2,32,1,128]{3,2,1,0:T(1,128)S(1)}, f32[2,32,1,128]{3,2,1,0:T(1,128)S(1)}, u32[]{:S(2)}, u32[]{:S(2)}) collective-permute-start(f32[2,32,1,128]{3,2,1,0:T(1,128)S(1)} %get-tuple-element.533), channel_id=1, source_target_pairs={{32,0},{64,32},{96,64},{128,96},{160,128},{192,160},{224,192},{256... | collective-permute-start | bytes 98312 | tf_op jit(solution)/shard_map/ppermute | solution.py:19
  15.3 143.6 %collective-permute-start.1 = (f32[2,32,1,128]{3,2,1,0:T(1,128)S(1)}, f32[2,32,1,128]{3,2,1,0:T(1,128)S(1)}, u32[]{:S(2)}, u32[]{:S(2)}) collective-permute-start(f32[2,32,1,128]{3,2,1,0:T(1,128)S(1)} %get-tuple-element.532), channel_id=1, source_target_pairs={{0,32},{32,64},{64,96},{96,128},{128,160},{160,192},{192,224},{224... | collective-permute-start | bytes 98312 | tf_op jit(solution)/shard_map/ppermute | solution.py:16
  150.6 20.1 %collective-permute-start.7 = (f32[2,32,10,1]{3,2,1,0:T(8,128)S(1)}, f32[2,32,10,1]{3,2,1,0:T(8,128)S(1)}, u32[]{:S(2)}, u32[]{:S(2)}) collective-permute-start(f32[2,32,10,1]{3,2,1,0:T(8,128)S(1)} %get-tuple-element.523), channel_id=1, source_target_pairs={{0,1},{1,2},{2,3},{3,4},{4,5},{5,6},{6,7},{7,8},{8,9},{9,10},{10,1... | collective-permute-start | bytes 7688 | tf_op jit(solution)/shard_map/ppermute | solution.py:16
  157.0 15.6 %collective-permute-start.6 = (f32[2,32,10,1]{3,2,1,0:T(8,128)S(1)}, f32[2,32,10,1]{3,2,1,0:T(8,128)S(1)}, u32[]{:S(2)}, u32[]{:S(2)}) collective-permute-start(f32[2,32,10,1]{3,2,1,0:T(8,128)S(1)} %get-tuple-element.522), channel_id=1, source_target_pairs={{1,0},{2,1},{3,2},{4,3},{5,4},{6,5},{7,6},{8,7},{9,8},{10,9},{11,1... | collective-permute-start | bytes 7688 | tf_op jit(solution)/shard_map/ppermute | solution.py:19
  160.7 429.4 %collective-permute-start.3 = (f32[2,32,10,1]{3,2,1,0:T(8,128)}, f32[2,32,10,1]{3,2,1,0:T(8,128)S(1)}, u32[]{:S(2)}, u32[]{:S(2)}) collective-permute-start(f32[2,32,10,1]{3,2,1,0:T(8,128)} %get-tuple-element.521), channel_id=1, source_target_pairs={{0,1},{1,2},{2,3},{3,4},{4,5},{5,6},{6,7},{7,8},{8,9},{9,10},{10,1... | collective-permute-start | bytes 7688 | tf_op jit(solution)/shard_map/ppermute | solution.py:16
  166.5 423.7 %collective-permute-start.2 = (f32[2,32,10,1]{3,2,1,0:T(8,128)}, f32[2,32,10,1]{3,2,1,0:T(8,128)S(1)}, u32[]{:S(2)}, u32[]{:S(2)}) collective-permute-start(f32[2,32,10,1]{3,2,1,0:T(8,128)} %get-tuple-element.520), channel_id=1, source_target_pairs={{1,0},{2,1},{3,2},{4,3},{5,4},{6,5},{7,6},{8,7},{9,8},{10,9},{11,1... | collective-permute-start | bytes 7688 | tf_op jit(solution)/shard_map/ppermute | solution.py:19
  173.7 4.6 copy-start.17
  173.7 6.3 copy-start.40
  186.8 6.3 copy-start.40
  199.8 6.3 copy-start.40
  212.7 4.5 copy-start.17
  212.8 6.3 copy-start.40
  225.7 4.5 copy-start.17
  225.7 6.3 copy-start.40
  238.7 6.3 copy-start.40
  251.7 6.3 copy-start.40
  264.7 6.3 copy-start.40
  277.7 4.5 copy-start.17
  277.7 6.3 copy-start.40
  290.7 4.5 copy-start.17
  290.7 6.3 copy-start.40
  303.7 6.3 copy-start.40
  316.7 6.3 copy-start.40
  329.7 6.3 copy-start.40
  342.7 4.5 copy-start.17
  342.7 6.3 copy-start.40
  355.7 4.5 copy-start.17
  355.7 6.3 copy-start.40
  368.7 6.3 copy-start.40
  381.7 6.3 copy-start.40
  394.7 4.5 copy-start.17
  394.7 6.3 copy-start.40
  407.6 4.5 copy-start.17
  407.7 6.3 copy-start.40
  420.6 4.5 copy-start.17
  420.6 6.3 copy-start.40
  433.6 6.3 copy-start.40
  446.6 6.3 copy-start.40
  459.6 4.5 copy-start.17
  459.6 6.3 copy-start.40
  472.6 4.5 copy-start.17
  472.6 6.3 copy-start.40
  485.6 6.3 copy-start.40
  498.6 6.3 copy-start.40
  511.6 6.3 copy-start.40
  524.6 4.5 copy-start.17
  524.6 6.3 copy-start.40
  537.6 6.3 copy-start.40
  550.6 6.3 copy-start.40
  563.6 4.6 copy-start.17
  563.6 6.3 copy-start.40
  576.6 4.6 copy-start.17
  576.6 6.3 copy-start.40
  591.3 311.9 %collective-permute-start.8 = (f32[2,32,1,128]{3,2,1,0:T(1,128)S(1)}, f32[2,32,1,128]{3,2,1,0:T(1,128)S(1)}, u32[]{:S(2)}, u32[]{:S(2)}) collective-permute-start(f32[2,32,1,128]{3,2,1,0:T(1,128)S(1)} %get-tuple-element.531), channel_id=1, source_target_pairs={{32,0},{64,32},{96,64},{128,96},{160,128},{192,160},{224,192},{256... | collective-permute-start | bytes 98312 | tf_op jit(solution)/shard_map/ppermute | solution.py:19
  592.6 310.6 %collective-permute-start.9 = (f32[2,32,1,128]{3,2,1,0:T(1,128)S(1)}, f32[2,32,1,128]{3,2,1,0:T(1,128)S(1)}, u32[]{:S(2)}, u32[]{:S(2)}) collective-permute-start(f32[2,32,1,128]{3,2,1,0:T(1,128)S(1)} %get-tuple-element.530), channel_id=1, source_target_pairs={{0,32},{32,64},{64,96},{96,128},{128,160},{160,192},{192,224},{224... | collective-permute-start | bytes 98312 | tf_op jit(solution)/shard_map/ppermute | solution.py:16
  903.6 16.7 %collective-permute-start.11 = (f32[2,32,10,1]{3,2,1,0:T(8,128)S(1)}, f32[2,32,10,1]{3,2,1,0:T(8,128)S(1)}, u32[]{:S(2)}, u32[]{:S(2)}) collective-permute-start(f32[2,32,10,1]{3,2,1,0:T(8,128)S(1)} %get-tuple-element.519), channel_id=1, source_target_pairs={{0,1},{1,2},{2,3},{3,4},{4,5},{5,6},{6,7},{7,8},{8,9},{9,10},{10,1... | collective-permute-start | bytes 7688 | tf_op jit(solution)/shard_map/ppermute | solution.py:16
  908.5 18.0 %collective-permute-start.10 = (f32[2,32,10,1]{3,2,1,0:T(8,128)S(1)}, f32[2,32,10,1]{3,2,1,0:T(8,128)S(1)}, u32[]{:S(2)}, u32[]{:S(2)}) collective-permute-start(f32[2,32,10,1]{3,2,1,0:T(8,128)S(1)} %get-tuple-element.518), channel_id=1, source_target_pairs={{1,0},{2,1},{3,2},{4,3},{5,4},{6,5},{7,6},{8,7},{9,8},{10,9},{11,1... | collective-permute-start | bytes 7688 | tf_op jit(solution)/shard_map/ppermute | solution.py:19
  (647 other events, 697.0 us)
where the time goes:
time: 941 us; the launch traced here: 928 us
  local copies, waits for them, and re-layouts  316 us (34%)
  matrix products  209 us (22%)
  loops' own time  189 us (20%)
  blocking collectives  105 us (11%)
  other arithmetic  46.2 us (5%)
  starting transfers between devices  41 us (4%)
  waiting for transfers between devices  19.7 us (2%)
    while x1920, local copies, waits for them, and re-layouts  250 us
    another operation x2, loops' own time, backward_lines(): lax.scan(backward_one_line, running, jnp.arange(solid.shape[0], dtype=jnp...  125 us
    psum x1, blocking collectives, shards(): lax.psum((running[0], running[1], running[2], running[3], running[4], run...  105 us
    another operation x1, loops' own time, forward_coupling(): lax.map(forward_one_line, jnp.arange(solid.shape[0], dtype=jnp.int32))  64.3 us
    dynamic_slice x96, local copies, waits for them, and re-layouts, forward_coupling(): lax.map(forward_one_line, jnp.arange(solid.shape[0], dtype=jnp.int32))  55.9 us
    dot_general x64, matrix products, backprop(): jnp.dot(w_out, d_logits, preferred_element_type=jnp.float32)  39.4 us
    dot_general x64, matrix products, network(): jnp.dot(w_in.T, features, preferred_element_type=jnp.float32)  35.9 us
    dot_general x64, matrix products, backprop(): jnp.dot(w_mid, d_hidden_two, preferred_element_type=jnp.float32)  33.9 us
  transfers between devices with their start and end apart: 12, of which 4 were waited for; matrix products, arithmetic and copies ran while one was open for 44% of the time, Pallas kernels for 0%

commit v1 on v0

--- a/solution.py
+++ b/solution.py
@@ -204,7 +204,8 @@
         + d_features
     )
     summed = lax.psum(
-        (running[0], running[1], running[2], running[3], running[4], running[5]), ("grp", "col")
+        lax.psum((running[0], running[1], running[2], running[3], running[4], running[5]), "col"),
+        "grp",
     )
     cell_count = solid_temp.size * lax.axis_size("grp") * lax.axis_size("col")
     scale = loss_gain / math.sqrt(cell_count)

time: 941 us -> 1030 us (1.095)
  the two profiles are of different devices: /device:TPU:19 before, /device:TPU:1 now
where the time goes in v1:
time: 1030 us; the launch traced here: 1020 us
  local copies, waits for them, and re-layouts  313 us (30%)
  matrix products  209 us (20%)
  loops' own time  189 us (18%)
  blocking collectives  188 us (18%)
  starting transfers between devices  55.7 us (5%)
  other arithmetic  46.3 us (4%)
  waiting for transfers between devices  16.2 us (2%)
    while x1920, local copies, waits for them, and re-layouts  247 us
    psum x1, blocking collectives, shards(): lax.psum((running[0], running[1], running[2], running[3], running[4], run...  133 us
    another operation x2, loops' own time, backward_lines(): lax.scan(backward_one_line, running, jnp.arange(solid.shape[0], dtype=jnp...  124 us
    another operation x1, loops' own time, forward_coupling(): lax.map(forward_one_line, jnp.arange(solid.shape[0], dtype=jnp.int32))  64.3 us
    dynamic_slice x96, local copies, waits for them, and re-layouts, forward_coupling(): lax.map(forward_one_line, jnp.arange(solid.shape[0], dtype=jnp.int32))  56 us
    psum x1, blocking collectives, shards(): lax.psum(lax.psum((running[0], running[1], running[2], running[3], runnin...  55.3 us
    ppermute x6, starting transfers between devices, padded_2(): lax.ppermute(lax.slice_in_dim(block, block.shape[dim] - width, None, axis...  39.8 us
    dot_general x64, matrix products, backprop(): jnp.dot(w_out, d_logits, preferred_element_type=jnp.float32)  39.7 us
  transfers between devices with their start and end apart: 12, of which 2 were waited for; matrix products, arithmetic and copies ran while one was open for 40% of the time, Pallas kernels for 0%

profile of v1, /device:TPU:1, one launch (start us, length us, event | category | flops | bytes accessed | tf_op | source)
XLA Modules:
  0.0 1018.6 jit_solution(4187620168065603818)
XLA Ops:
  0.7 1.2 fusion.89
  1.9 1.3 collective-permute-start.4
  3.2 4.6 collective-permute-start.5
  9.1 2.7 add_bitcast_fusion.1
  11.8 2.7 add_bitcast_fusion
  14.7 1.3 collective-permute-start
  16.0 4.9 collective-permute-start.1
  21.7 128.7 %while.59 = (s32[]{:T(128)}, f32[32,8,128]{2,1,0:T(8,128)S(1)}, s32[32]{0:T(128)S(1)}, bf16[10,32,8,128]{3,2,1,0:T(8,128)(2,1)}, bf16[32,8,128]{2,1,0:T(8,128)(2...) while((s32[]{:T(128)}, f32[32,8,128]{2,1,0:T(8,128)S(1)}, ...), condition=%wide.region_1.2_spmd, body=%wide.region_0.1_spmd.sunk | while | flops 10574853 | bytes 510433 | solution.py:110
  151.4 5.6 collective-permute-start.7
  157.1 4.0 collective-permute-start.6
  161.7 1.2 fusion.96
  162.9 2.4 collective-permute-start.3
  165.3 1.9 collective-permute-start.2
  167.3 7.1 collective-permute-done.6
  175.6 413.0 %while.61 = (s32[]{:T(128)}, f32[12,64]{1,0:T(8,128)S(1)}, f32[64]{0:T(128)}, f32[64,64]{1,0:T(8,128)S(1)}, f32[64]{0:T(128)}, /*index=5*/f32[64,2]{0,1:T(2,128)...) while((s32[]{:T(128)}, f32[12,64]{1,0:T(8,128)S(1)}, ...), condition=%wide.region_6.7_spmd.clone, body=%wide.region_2.6_spmd.clone.sunk | while | flops 30749576 | bytes 3280900 | solution.py:130
  179.1 0.9 fusion.247
  181.8 0.9 convert_reduce_fusion.16
  194.7 0.9 convert_reduce_fusion.16
  204.9 0.9 fusion.247
  207.6 0.9 convert_reduce_fusion.16
  220.5 0.9 convert_reduce_fusion.16
  230.8 0.9 fusion.247
  233.4 0.9 convert_reduce_fusion.16
  243.7 0.9 fusion.247
  246.3 0.9 convert_reduce_fusion.16
  259.2 0.9 convert_reduce_fusion.16
  269.5 0.9 fusion.247
  272.1 0.9 convert_reduce_fusion.16
  282.4 0.9 fusion.247
  285.0 0.9 convert_reduce_fusion.16
  297.9 0.9 convert_reduce_fusion.16
  308.2 0.9 fusion.247
  310.8 0.9 convert_reduce_fusion.16
  321.1 0.9 fusion.247
  323.7 0.9 convert_reduce_fusion.16
  336.6 0.9 convert_reduce_fusion.16
  346.9 0.9 fusion.247
  349.6 0.9 convert_reduce_fusion.16
  362.5 0.9 convert_reduce_fusion.16
  375.4 0.9 convert_reduce_fusion.16
  388.3 0.9 convert_reduce_fusion.16
  401.2 0.9 convert_reduce_fusion.16
  414.1 0.9 convert_reduce_fusion.16
  427.0 0.9 convert_reduce_fusion.16
  439.9 0.9 convert_reduce_fusion.16
  452.8 0.9 convert_reduce_fusion.16
  465.7 0.9 convert_reduce_fusion.16
  478.6 0.9 convert_reduce_fusion.16
  491.5 0.9 convert_reduce_fusion.16
  504.4 0.9 convert_reduce_fusion.16
  517.3 0.9 convert_reduce_fusion.16
  530.2 0.9 convert_reduce_fusion.16
  543.1 0.9 convert_reduce_fusion.16
  556.0 0.9 convert_reduce_fusion.16
  568.9 0.9 convert_reduce_fusion.16
  581.9 0.9 convert_reduce_fusion.16
  590.3 1.3 collective-permute-start.8
  591.6 4.0 collective-permute-start.9
  596.4 195.9 %while.60 = (s32[]{:T(128)}, f32[12,64]{1,0:T(8,128)S(1)}, f32[64]{0:T(128)S(1)}, f32[64,64]{1,0:T(8,128)S(1)}, f32[64]{0:T(128)S(1)}, /*index=5*/f32[64,2]{0,1:...) while((s32[]{:T(128)}, f32[12,64]{1,0:T(8,128)S(1)}, ...), condition=%wide.region_11.12_spmd, body=%wide.region_7.11_spmd.sunk | while | flops 30744452 | bytes 2216265 | solution.py:130
  792.4 132.7 %all-reduce = (f32[12,64]{1,0:T(8,128)S(1)}, f32[64]{0:T(128)S(1)}, f32[64,64]{1,0:T(8,128)S(1)}, f32[64]{0:T(128)S(1)}, f32[64,2]{0,1:T(2,128)S(1)}, /*index=5*/f32[2]{0:T(128)S(1)}) all-reduce(f32[12,64]{1,0:T(8,128)S(1)} %get-tuple-element.299, f32[64]{0:T(128)S(1)} %get-tuple-element.300, ...), channel_id=1, replica_groups=mesh['grp'=16,'col'=32] {'col'}, use_global_device_ids=true, to_apply=%region_12.13 | all-reduce | flops 5122 | bytes 40976 | tf_op jit(solution)/shard_map/psum | solution.py:207
  925.1 55.3 %all-reduce.1 = (f32[12,64]{1,0:T(8,128)S(1)}, f32[64]{0:T(128)S(1)}, f32[64,64]{1,0:T(8,128)S(1)}, f32[64]{0:T(128)S(1)}, f32[64,2]{0,1:T(2,128)S(1)}, /*index=5*/f32[2]{0:T(128)S(1)}) all-reduce(f32[12,64]{1,0:T(8,128)S(1)} %get-tuple-element.472, f32[64]{0:T(128)S(1)} %get-tuple-element.473, ...), channel_id=1, replica_groups=mesh['grp'=16,'col'=32] {'grp'}, use_global_device_ids=true, to_apply=%region_13.14 | all-reduce | flops 5122 | bytes 40976 | tf_op jit(solution)/shard_map/psum | solution.py:206
  983.5 18.3 %collective-permute-start.11 = (f32[2,32,10,1]{3,2,1,0:T(8,128)S(1)}, f32[2,32,10,1]{3,2,1,0:T(8,128)S(1)}, u32[]{:S(2)}, u32[]{:S(2)}) collective-permute-start(f32[2,32,10,1]{3,2,1,0:T(8,128)S(1)} %get-tuple-element.525), channel_id=1, source_target_pairs={{0,1},{1,2},{2,3},{3,4},{4,5},{5,6},{6,7},{7,8},{8,9},{9,10},{10,1... | collective-permute-start | bytes 7688 | tf_op jit(solution)/shard_map/ppermute | solution.py:16
  1001.8 6.1 collective-permute-start.10
  1008.4 9.1 collective-permute-done.10
  (3297 shorter events, 523.9 us)
Async XLA Ops:
  0.6 8.4 copy-start.7
  0.6 8.4 copy-start.8
  1.8 6.0 copy-start.31
  1.9 149.3 %collective-permute-start.4 = (f32[2,32,1,128]{3,2,1,0:T(1,128)S(1)}, f32[2,32,1,128]{3,2,1,0:T(1,128)S(1)}, u32[]{:S(2)}, u32[]{:S(2)}) collective-permute-start(f32[2,32,1,128]{3,2,1,0:T(1,128)S(1)} %get-tuple-element.543), channel_id=1, source_target_pairs={{32,0},{64,32},{96,64},{128,96},{160,128},{192,160},{224,192},{256... | collective-permute-start | bytes 98312 | tf_op jit(solution)/shard_map/ppermute | solution.py:19
  3.2 148.0 %collective-permute-start.5 = (f32[2,32,1,128]{3,2,1,0:T(1,128)S(1)}, f32[2,32,1,128]{3,2,1,0:T(1,128)S(1)}, u32[]{:S(2)}, u32[]{:S(2)}) collective-permute-start(f32[2,32,1,128]{3,2,1,0:T(1,128)S(1)} %get-tuple-element.542), channel_id=1, source_target_pairs={{0,32},{32,64},{64,96},{96,128},{128,160},{160,192},{192,224},{224... | collective-permute-start | bytes 98312 | tf_op jit(solution)/shard_map/ppermute | solution.py:16
  14.5 6.3 copy-start.1
  14.6 6.3 copy-start
  14.7 146.4 %collective-permute-start = (f32[2,32,1,128]{3,2,1,0:T(1,128)S(1)}, f32[2,32,1,128]{3,2,1,0:T(1,128)S(1)}, u32[]{:S(2)}, u32[]{:S(2)}) collective-permute-start(f32[2,32,1,128]{3,2,1,0:T(1,128)S(1)} %get-tuple-element.539), channel_id=1, source_target_pairs={{32,0},{64,32},{96,64},{128,96},{160,128},{192,160},{224,192},{256... | collective-permute-start | bytes 98312 | tf_op jit(solution)/shard_map/ppermute | solution.py:19
  16.0 145.1 %collective-permute-start.1 = (f32[2,32,1,128]{3,2,1,0:T(1,128)S(1)}, f32[2,32,1,128]{3,2,1,0:T(1,128)S(1)}, u32[]{:S(2)}, u32[]{:S(2)}) collective-permute-start(f32[2,32,1,128]{3,2,1,0:T(1,128)S(1)} %get-tuple-element.538), channel_id=1, source_target_pairs={{0,32},{32,64},{64,96},{96,128},{128,160},{160,192},{192,224},{224... | collective-permute-start | bytes 98312 | tf_op jit(solution)/shard_map/ppermute | solution.py:16
  151.4 15.8 %collective-permute-start.7 = (f32[2,32,10,1]{3,2,1,0:T(8,128)S(1)}, f32[2,32,10,1]{3,2,1,0:T(8,128)S(1)}, u32[]{:S(2)}, u32[]{:S(2)}) collective-permute-start(f32[2,32,10,1]{3,2,1,0:T(8,128)S(1)} %get-tuple-element.529), channel_id=1, source_target_pairs={{0,1},{1,2},{2,3},{3,4},{4,5},{5,6},{6,7},{7,8},{8,9},{9,10},{10,1... | collective-permute-start | bytes 7688 | tf_op jit(solution)/shard_map/ppermute | solution.py:16
  157.1 17.3 %collective-permute-start.6 = (f32[2,32,10,1]{3,2,1,0:T(8,128)S(1)}, f32[2,32,10,1]{3,2,1,0:T(8,128)S(1)}, u32[]{:S(2)}, u32[]{:S(2)}) collective-permute-start(f32[2,32,10,1]{3,2,1,0:T(8,128)S(1)} %get-tuple-element.528), channel_id=1, source_target_pairs={{1,0},{2,1},{3,2},{4,3},{5,4},{6,5},{7,6},{8,7},{9,8},{10,9},{11,1... | collective-permute-start | bytes 7688 | tf_op jit(solution)/shard_map/ppermute | solution.py:19
  162.9 426.2 %collective-permute-start.3 = (f32[2,32,10,1]{3,2,1,0:T(8,128)}, f32[2,32,10,1]{3,2,1,0:T(8,128)S(1)}, u32[]{:S(2)}, u32[]{:S(2)}) collective-permute-start(f32[2,32,10,1]{3,2,1,0:T(8,128)} %get-tuple-element.527), channel_id=1, source_target_pairs={{0,1},{1,2},{2,3},{3,4},{4,5},{5,6},{6,7},{7,8},{8,9},{9,10},{10,1... | collective-permute-start | bytes 7688 | tf_op jit(solution)/shard_map/ppermute | solution.py:16
  165.3 423.7 %collective-permute-start.2 = (f32[2,32,10,1]{3,2,1,0:T(8,128)}, f32[2,32,10,1]{3,2,1,0:T(8,128)S(1)}, u32[]{:S(2)}, u32[]{:S(2)}) collective-permute-start(f32[2,32,10,1]{3,2,1,0:T(8,128)} %get-tuple-element.526), channel_id=1, source_target_pairs={{1,0},{2,1},{3,2},{4,3},{5,4},{6,5},{7,6},{8,7},{9,8},{10,9},{11,1... | collective-permute-start | bytes 7688 | tf_op jit(solution)/shard_map/ppermute | solution.py:19
  175.6 4.5 copy-start.17
  175.6 6.2 copy-start.40
  188.5 6.2 copy-start.40
  201.4 4.5 copy-start.17
  201.4 6.2 copy-start.40
  214.3 6.2 copy-start.40
  227.2 4.5 copy-start.17
  227.2 6.2 copy-start.40
  240.1 4.5 copy-start.17
  240.1 6.2 copy-start.40
  253.0 6.2 copy-start.40
  265.9 4.5 copy-start.17
  265.9 6.2 copy-start.40
  278.8 4.5 copy-start.17
  278.8 6.2 copy-start.40
  291.7 6.2 copy-start.40
  304.6 4.5 copy-start.17
  304.6 6.2 copy-start.40
  317.5 4.5 copy-start.17
  317.5 6.2 copy-start.40
  330.4 6.2 copy-start.40
  343.3 4.5 copy-start.17
  343.3 6.2 copy-start.40
  356.2 4.5 copy-start.17
  356.3 6.2 copy-start.40
  369.2 6.2 copy-start.40
  382.1 4.5 copy-start.17
  382.1 6.2 copy-start.40
  395.0 4.5 copy-start.17
  395.0 6.2 copy-start.40
  407.9 6.2 copy-start.40
  420.8 4.5 copy-start.17
  420.8 6.2 copy-start.40
  433.7 6.2 copy-start.40
  446.6 6.2 copy-start.40
  459.5 6.2 copy-start.40
  472.4 6.2 copy-start.40
  485.3 6.2 copy-start.40
  498.2 6.2 copy-start.40
  511.1 6.2 copy-start.40
  524.0 6.2 copy-start.40
  536.9 6.2 copy-start.40
  549.8 6.2 copy-start.40
  562.7 4.5 copy-start.17
  562.7 6.2 copy-start.40
  575.6 4.5 copy-start.17
  575.6 6.2 copy-start.40
  590.3 392.9 %collective-permute-start.8 = (f32[2,32,1,128]{3,2,1,0:T(1,128)S(1)}, f32[2,32,1,128]{3,2,1,0:T(1,128)S(1)}, u32[]{:S(2)}, u32[]{:S(2)}) collective-permute-start(f32[2,32,1,128]{3,2,1,0:T(1,128)S(1)} %get-tuple-element.537), channel_id=1, source_target_pairs={{32,0},{64,32},{96,64},{128,96},{160,128},{192,160},{224,192},{256... | collective-permute-start | bytes 98312 | tf_op jit(solution)/shard_map/ppermute | solution.py:19
  591.6 391.6 %collective-permute-start.9 = (f32[2,32,1,128]{3,2,1,0:T(1,128)S(1)}, f32[2,32,1,128]{3,2,1,0:T(1,128)S(1)}, u32[]{:S(2)}, u32[]{:S(2)}) collective-permute-start(f32[2,32,1,128]{3,2,1,0:T(1,128)S(1)} %get-tuple-element.536), channel_id=1, source_target_pairs={{0,32},{32,64},{64,96},{96,128},{128,160},{160,192},{192,224},{224... | collective-permute-start | bytes 98312 | tf_op jit(solution)/shard_map/ppermute | solution.py:16
  983.5 24.9 %collective-permute-start.11 = (f32[2,32,10,1]{3,2,1,0:T(8,128)S(1)}, f32[2,32,10,1]{3,2,1,0:T(8,128)S(1)}, u32[]{:S(2)}, u32[]{:S(2)}) collective-permute-start(f32[2,32,10,1]{3,2,1,0:T(8,128)S(1)} %get-tuple-element.525), channel_id=1, source_target_pairs={{0,1},{1,2},{2,3},{3,4},{4,5},{5,6},{6,7},{7,8},{8,9},{9,10},{10,1... | collective-permute-start | bytes 7688 | tf_op jit(solution)/shard_map/ppermute | solution.py:16
  1001.8 15.7 %collective-permute-start.10 = (f32[2,32,10,1]{3,2,1,0:T(8,128)S(1)}, f32[2,32,10,1]{3,2,1,0:T(8,128)S(1)}, u32[]{:S(2)}, u32[]{:S(2)}) collective-permute-start(f32[2,32,10,1]{3,2,1,0:T(8,128)S(1)} %get-tuple-element.524), channel_id=1, source_target_pairs={{1,0},{2,1},{3,2},{4,3},{5,4},{6,5},{7,6},{8,7},{9,8},{10,9},{11,1... | collective-permute-start | bytes 7688 | tf_op jit(solution)/shard_map/ppermute | solution.py:19
  (647 other events, 687.4 us)
